TPU v7x, 32 devices: a whole 2x2x4 slice. The times are simulated.
32 devices in a mesh: dp: 16 (over z, y, x), tensor: 2 (over core).
Axes of the slice: x: 2, y: 2, z: 4, core: 2. Of those that a mesh axis runs over, the one named last changes fastest.
Arguments:
- tokens: bfloat16 [16384, 768], P('dp'), may hold values from -6 to 6
- cotangent: bfloat16 [16384, 768], P('dp'), may hold values from -6 to 6
- lengths: int32 [32], P('dp'), may hold values from 113 to 512, as said below
- proj_weight: float32 [2, 768, 3, 768], P(None, 'dp', None, 'tensor'), may hold values from -0.21875 to 0.21875
- out_weight: float32 [2, 768, 768], P(None, 'dp', 'tensor'), may hold values from -0.875 to 0.875
- up_weight: float32 [2, 768, 3072], P(None, 'dp', 'tensor'), may hold values from -0.21875 to 0.21875
- down_weight: float32 [2, 768, 3072], P(None, 'dp', 'tensor'), may hold values from -0.109375 to 0.109375
- small_params: float32 [2, 8448], replicated, may hold values from -0.8 to 1.4
- proj_first: float32 [2, 768, 3, 768], P(None, 'dp', None, 'tensor'), may hold values from -0.00018310547 to 0.00018310547
- proj_second: float32 [2, 768, 3, 768], P(None, 'dp', None, 'tensor'), may hold values from 3.527916e-11 to 3.52791626e-09
- out_first: float32 [2, 768, 768], P(None, 'dp', 'tensor'), may hold values from -0.00018310547 to 0.00018310547
- out_second: float32 [2, 768, 768], P(None, 'dp', 'tensor'), may hold values from 7.0558325e-12 to 7.0558325e-10
- up_first: float32 [2, 768, 3072], P(None, 'dp', 'tensor'), may hold values from -0.00018310547 to 0.00018310547
- up_second: float32 [2, 768, 3072], P(None, 'dp', 'tensor'), may hold values from 3.527916e-11 to 3.52791626e-09
- down_first: float32 [2, 768, 3072], P(None, 'dp', 'tensor'), may hold values from -0.00018310547 to 0.00018310547
- down_second: float32 [2, 768, 3072], P(None, 'dp', 'tensor'), may hold values from 3.527916e-11 to 3.52791626e-09
- small_first: float32 [2, 8448], replicated, may hold values from -0.00018310547 to 0.00018310547
- small_second: float32 [2, 8448], replicated, may hold values from 3.527916e-11 to 5.644666e-10
Outputs:
- activations: float32 [16384, 768], P('dp')
- input_grad: float32 [16384, 768], P('dp')
- grad_norm: float32 [], replicated
- proj_first_new: float32 [2, 768, 3, 768], P(None, 'dp', None, 'tensor')
- proj_second_new: float32 [2, 768, 3, 768], P(None, 'dp', None, 'tensor')
- proj_weight_new: float32 [2, 768, 3, 768], P(None, 'dp', None, 'tensor')
- out_first_new: float32 [2, 768, 768], P(None, 'dp', 'tensor')
- out_second_new: float32 [2, 768, 768], P(None, 'dp', 'tensor')
- out_weight_new: float32 [2, 768, 768], P(None, 'dp', 'tensor')
- up_first_new: float32 [2, 768, 3072], P(None, 'dp', 'tensor')
- up_second_new: float32 [2, 768, 3072], P(None, 'dp', 'tensor')
- up_weight_new: float32 [2, 768, 3072], P(None, 'dp', 'tensor')
- down_first_new: float32 [2, 768, 3072], P(None, 'dp', 'tensor')
- down_second_new: float32 [2, 768, 3072], P(None, 'dp', 'tensor')
- down_weight_new: float32 [2, 768, 3072], P(None, 'dp', 'tensor')
- small_first_new: float32 [2, 8448], replicated
- small_second_new: float32 [2, 8448], replicated
- small_params_new: float32 [2, 8448], replicated
Inputs may be any that keep to these rules, and one draw needn't show every extreme that they name: `lengths`: each length is 512, 256 or 128, reduced by less than max(1, 16); the first sequence has length 512.
All inputs are finite; a program needn't handle non-finite values.
Results may differ from a plain program's by a relative error of at most 0.03.
The roundings to bfloat16 on the way count: a program that leaves them out, or rounds other values in their place, can miss the bound.
Values may be sent and summed in bfloat16 or wider, within the bound.
No kernel may reach another device: no remote copies, remote signals or barrier semaphores. Data moves between devices by JAX's collectives and lax.ppermute only.
A program may use at most 192 MiB of HBM per device.

v0:
```python
from functools import partial
import math
import jax
import jax.numpy as jnp
from jax import lax
from jax.sharding import PartitionSpec as P

D = 768
HEADS = 12
FF = 3072
beta_one = 0.9
beta_two = 0.999
adam_eps = 1e-06
decay_rate = 0.01
matrix_rate = 1.0
vector_rate = 0.3
clip_norm = 1.0
step_count = 10.0
norm_eps = 1e-06
masked_score = -1e30


def layer_norm(values, norm_gain, norm_shift):
    average = jnp.mean(values, axis=-1, keepdims=True)
    centered = values - average
    variance = jnp.mean(centered * centered, axis=-1, keepdims=True)
    return centered * lax.rsqrt(variance + norm_eps) * norm_gain + norm_shift


def split_vector(packed):
    bounds = [0, D, 2 * D, 2 * D + FF, 3 * D + FF, 4 * D + FF, 5 * D + FF, 6 * D + FF, 7 * D + FF]
    return [packed[bounds[place] : bounds[place + 1]] for place in range(8)]


def head_scores(query, keys, score_scale):
    return jnp.einsum("qhe,khe->hqk", query, keys, preferred_element_type=jnp.float32) * score_scale


def total_scores(pairs, score_scale):
    score_total = head_scores(pairs[0], pairs[1], score_scale)
    for place in range(2, len(pairs), 2):
        score_total = score_total + head_scores(pairs[place], pairs[place + 1], score_scale)
    return score_total


def attend_forward(block_item, score_scale):
    key_valid, value_rows = (block_item[0], block_item[1])
    score_total = total_scores(block_item[2:], score_scale)
    masked = jnp.where(key_valid[None, None, :], score_total, masked_score)
    row_max = jnp.max(masked, axis=-1, keepdims=True)
    exp_terms = jnp.exp(masked - row_max)
    row_sum = jnp.sum(exp_terms, axis=-1, keepdims=True)
    soft_low = (exp_terms / row_sum).astype(jnp.bfloat16)
    context = jnp.einsum("hqk,khe->qhe", soft_low, value_rows, preferred_element_type=jnp.float32)
    return (context.astype(jnp.bfloat16), (row_max + jnp.log(row_sum))[..., 0])


def attend_backward(block_item, score_scale, with_later, keep_total):
    key_valid, value_rows, log_norm, context_grad = (
        block_item[0],
        block_item[1],
        block_item[2],
        block_item[3],
    )
    rest = block_item[4:]
    if with_later:
        later = rest[0]
        pairs = rest[1:]
    else:
        pairs = rest
    score_total = total_scores(pairs, score_scale)
    soft = jnp.where(key_valid[None, None, :], jnp.exp(score_total - log_norm[..., None]), 0.0)
    soft_grad = jnp.einsum(
        "qhe,khe->hqk", context_grad, value_rows, preferred_element_type=jnp.float32
    )
    total_grad = soft * (soft_grad - jnp.sum(soft * soft_grad, axis=-1, keepdims=True))
    if with_later:
        total_grad = total_grad + later
    total_low = total_grad.astype(jnp.bfloat16)
    query_grad = (
        jnp.einsum("hqk,khe->qhe", total_low, pairs[1], preferred_element_type=jnp.float32)
        * score_scale
    )
    key_grad = (
        jnp.einsum("hqk,qhe->khe", total_low, pairs[0], preferred_element_type=jnp.float32)
        * score_scale
    )
    value_grad = jnp.einsum(
        "hqk,qhe->khe", soft.astype(jnp.bfloat16), context_grad, preferred_element_type=jnp.float32
    )
    results = (query_grad, key_grad, value_grad)
    if keep_total:
        results = results + (total_grad,)
    return results


def adam_parts(gradient, first, second, factor):
    clipped = gradient * factor
    first_new = beta_one * first + (1.0 - beta_one) * clipped
    second_new = beta_two * second + (1.0 - beta_two) * clipped * clipped
    first_hat = first_new / (1.0 - beta_one**step_count)
    second_hat = second_new / (1.0 - beta_two**step_count)
    return (first_new, second_new, first_hat / (jnp.sqrt(second_hat) + adam_eps))


def local(
    tokens,
    cotangent,
    lengths,
    proj_weight,
    out_weight,
    up_weight,
    down_weight,
    small_params,
    proj_first,
    proj_second,
    out_first,
    out_second,
    up_first,
    up_second,
    down_first,
    down_second,
    small_first,
    small_second,
):
    layers = proj_weight.shape[0]
    seq_count = lengths.shape[0]
    seq_len = tokens.shape[0] // seq_count
    local_width = proj_weight.shape[3]
    head_dim = D // HEADS
    local_heads = local_width // head_dim
    hidden_local = up_weight.shape[2]
    score_scale = 1.0 / math.sqrt(head_dim)
    share_scale = 1.0 / lax.axis_size("tensor")
    tensor_rank = lax.axis_index("tensor")
    proj_full, out_full, up_full, down_full = (
        lax.all_gather(proj_weight.astype(jnp.bfloat16), "dp", axis=1, tiled=True),
        lax.all_gather(out_weight.astype(jnp.bfloat16), "dp", axis=1, tiled=True),
        lax.all_gather(up_weight.astype(jnp.bfloat16), "dp", axis=1, tiled=True),
        lax.all_gather(down_weight.astype(jnp.bfloat16), "dp", axis=1, tiled=True),
    )
    positions = jnp.arange(seq_len)
    key_valid = positions[None, :] < lengths[:, None]
    row_valid = key_valid.reshape(-1, 1)

    def own_part(vector, width):
        return lax.dynamic_slice_in_dim(vector, tensor_rank * width, width)

    def place_part(local_values, full_width):
        return lax.dynamic_update_slice_in_dim(
            jnp.zeros((full_width,), jnp.float32),
            local_values,
            tensor_rank * local_values.shape[0],
            0,
        )

    def heads_view(rows):
        return rows.reshape(seq_count, seq_len, local_heads, head_dim)

    hidden = tokens.astype(jnp.float32)
    saved = []
    for layer_at in range(layers):
        bias_v, bias_o, bias_up, bias_down, gain_one, shift_one, gain_two, shift_two = split_vector(
            small_params[layer_at]
        )
        input_low = hidden.astype(jnp.bfloat16)
        projected = jnp.einsum(
            "td,dcf->tcf", input_low, proj_full[layer_at], preferred_element_type=jnp.float32
        )
        query_low = projected[:, 0].astype(jnp.bfloat16)
        key_low = projected[:, 1].astype(jnp.bfloat16)
        value_low = (projected[:, 2] + own_part(bias_v, local_width)).astype(jnp.bfloat16)
        pairs = [heads_view(query_low), heads_view(key_low)]
        for earlier in reversed(saved):
            pairs += [heads_view(earlier["query"]), heads_view(earlier["keys"])]
        context_low, log_norm = lax.map(
            partial(attend_forward, score_scale=score_scale),
            (key_valid, heads_view(value_low)) + tuple(pairs),
        )
        context_low = context_low.reshape(-1, local_width)
        attended = lax.psum(
            jnp.einsum(
                "tf,df->td", context_low, out_full[layer_at], preferred_element_type=jnp.float32
            ).astype(jnp.bfloat16),
            "tensor",
        ).astype(jnp.float32)
        first_in = hidden + attended + bias_o
        first_out = layer_norm(first_in, gain_one, shift_one)
        first_low = first_out.astype(jnp.bfloat16)
        before_act = jnp.einsum(
            "td,df->tf", first_low, up_full[layer_at], preferred_element_type=jnp.float32
        ) + own_part(bias_up, hidden_local)
        act_low = jax.nn.gelu(before_act, approximate=False).astype(jnp.bfloat16)
        returned = lax.psum(
            jnp.einsum(
                "tf,df->td", act_low, down_full[layer_at], preferred_element_type=jnp.float32
            ).astype(jnp.bfloat16),
            "tensor",
        ).astype(jnp.float32)
        second_in = first_out + returned + bias_down
        saved.append(
            {
                "layer_input": input_low,
                "query": query_low,
                "keys": key_low,
                "value_rows": value_low,
                "log_norm": log_norm,
                "context": context_low,
                "first_in": first_in,
                "first_low": first_low,
                "before_act": before_act,
                "act_low": act_low,
                "second_in": second_in,
            }
        )
        hidden = layer_norm(second_in, gain_two, shift_two)
    grad_rows = jnp.where(row_valid, cotangent.astype(jnp.float32), 0.0)
    proj_grads = [None] * layers
    out_grads = [None] * layers
    up_grads = [None] * layers
    down_grads = [None] * layers
    small_grads = [None] * layers
    later_total = None
    for layer_at in reversed(range(layers)):
        kept = saved[layer_at]
        bias_v, bias_o, bias_up, bias_down, gain_one, shift_one, gain_two, shift_two = split_vector(
            small_params[layer_at]
        )
        second_in_grad, gain_two_grad, shift_two_grad = jax.vjp(
            layer_norm, kept["second_in"], gain_two, shift_two
        )[1](grad_rows)
        down_in_low = second_in_grad.astype(jnp.bfloat16)
        down_grads[layer_at] = jnp.einsum(
            "td,tf->df", down_in_low, kept["act_low"], preferred_element_type=jnp.float32
        )
        act_grad = jnp.einsum(
            "td,df->tf", down_in_low, down_full[layer_at], preferred_element_type=jnp.float32
        )
        before_grad = jax.vjp(partial(jax.nn.gelu, approximate=False), kept["before_act"])[1](
            act_grad
        )[0]
        before_low = before_grad.astype(jnp.bfloat16)
        up_grads[layer_at] = jnp.einsum(
            "td,tf->df", kept["first_low"], before_low, preferred_element_type=jnp.float32
        )
        first_back = lax.psum(
            jnp.einsum(
                "tf,df->td", before_low, up_full[layer_at], preferred_element_type=jnp.float32
            ).astype(jnp.bfloat16),
            "tensor",
        ).astype(jnp.float32)
        first_out_grad = second_in_grad + first_back
        first_in_grad, gain_one_grad, shift_one_grad = jax.vjp(
            layer_norm, kept["first_in"], gain_one, shift_one
        )[1](first_out_grad)
        out_in_low = first_in_grad.astype(jnp.bfloat16)
        out_grads[layer_at] = jnp.einsum(
            "td,tf->df", out_in_low, kept["context"], preferred_element_type=jnp.float32
        )
        context_grad = jnp.einsum(
            "td,df->tf", out_in_low, out_full[layer_at], preferred_element_type=jnp.float32
        ).astype(jnp.bfloat16)
        pairs = [heads_view(kept["query"]), heads_view(kept["keys"])]
        for earlier in reversed(saved[:layer_at]):
            pairs += [heads_view(earlier["query"]), heads_view(earlier["keys"])]
        items = (
            key_valid,
            heads_view(kept["value_rows"]),
            kept["log_norm"],
            heads_view(context_grad),
        )
        with_later = later_total is not None
        if with_later:
            items = items + (later_total,)
        items = items + tuple(pairs)
        results = lax.map(
            partial(
                attend_backward,
                score_scale=score_scale,
                with_later=with_later,
                keep_total=layer_at > 0,
            ),
            items,
        )
        later_total = results[3] if layer_at > 0 else None
        query_grad = results[0].reshape(-1, local_width)
        key_grad = results[1].reshape(-1, local_width)
        value_grad = results[2].reshape(-1, local_width)
        proj_grad_low = jnp.stack([query_grad, key_grad, value_grad], axis=1).astype(jnp.bfloat16)
        proj_grads[layer_at] = jnp.einsum(
            "td,tcf->dcf", kept["layer_input"], proj_grad_low, preferred_element_type=jnp.float32
        )
        input_back = lax.psum(
            jnp.einsum(
                "tcf,dcf->td",
                proj_grad_low,
                proj_full[layer_at],
                preferred_element_type=jnp.float32,
            ).astype(jnp.bfloat16),
            "tensor",
        ).astype(jnp.float32)
        grad_rows = first_in_grad + input_back
        small_grads[layer_at] = jnp.concatenate(
            [
                place_part(jnp.sum(value_grad, axis=0), D),
                share_scale * jnp.sum(first_in_grad, axis=0),
                place_part(jnp.sum(before_grad, axis=0), FF),
                share_scale * jnp.sum(second_in_grad, axis=0),
                share_scale * gain_one_grad,
                share_scale * shift_one_grad,
                share_scale * gain_two_grad,
                share_scale * shift_two_grad,
            ]
        )
    big_totals = (
        jnp.stack(proj_grads),
        jnp.stack(out_grads),
        jnp.stack(up_grads),
        jnp.stack(down_grads),
    )
    small_partial = jnp.stack(small_grads)
    row_count = proj_weight.shape[1]
    summed = lax.psum((big_totals[0], big_totals[1], big_totals[2], big_totals[3]), "dp")
    row_start = lax.axis_index("dp") * row_count
    shares = tuple(
        (lax.dynamic_slice_in_dim(summed_part, row_start, row_count, 1) for summed_part in summed)
    )
    masters = (proj_weight, out_weight, up_weight, down_weight)
    firsts = (proj_first, out_first, up_first, down_first)
    seconds = (proj_second, out_second, up_second, down_second)
    square_part = jnp.sum(shares[0] * shares[0])
    for kind_at in range(1, 4):
        square_part = square_part + jnp.sum(shares[kind_at] * shares[kind_at])
    weight_square = jnp.stack(
        [jnp.sum(master * master, axis=tuple(range(1, master.ndim))) for master in masters]
    )
    square_big, weight_square, small_grad = lax.psum(
        (square_part, weight_square, small_partial), ("dp", "tensor")
    )
    grad_norm = jnp.sqrt(square_big + jnp.sum(small_grad * small_grad))
    factor = clip_norm / jnp.maximum(grad_norm, clip_norm)
    moments = []
    updates = []
    for kind_at in range(4):
        first_new, second_new, direction = adam_parts(
            shares[kind_at], firsts[kind_at], seconds[kind_at], factor
        )
        moments.append((first_new, second_new))
        updates.append(direction + decay_rate * masters[kind_at])
    update_square = jnp.stack(
        [jnp.sum(update * update, axis=tuple(range(1, update.ndim))) for update in updates]
    )
    update_square = lax.psum(update_square, ("dp", "tensor"))
    ratio = jnp.sqrt(weight_square) / jnp.sqrt(update_square)
    outputs = [hidden, grad_rows, grad_norm]
    for kind_at in range(4):
        master = masters[kind_at]
        scaled = ratio[kind_at].reshape((-1,) + (1,) * (master.ndim - 1))
        outputs += [
            moments[kind_at][0],
            moments[kind_at][1],
            master - matrix_rate * scaled * updates[kind_at],
        ]
    small_first_new, small_second_new, small_direction = adam_parts(
        small_grad, small_first, small_second, factor
    )
    outputs += [small_first_new, small_second_new, small_params - vector_rate * small_direction]
    return tuple(outputs)


def solution(mesh):
    placed = (
        P("dp", None),
        P("dp", None),
        P("dp"),
        P(None, "dp", None, "tensor"),
        P(None, "dp", "tensor"),
        P(None, "dp", "tensor"),
        P(None, "dp", "tensor"),
        P(),
        P(None, "dp", None, "tensor"),
        P(None, "dp", None, "tensor"),
        P(None, "dp", "tensor"),
        P(None, "dp", "tensor"),
        P(None, "dp", "tensor"),
        P(None, "dp", "tensor"),
        P(None, "dp", "tensor"),
        P(None, "dp", "tensor"),
        P(),
        P(),
    )
    return jax.shard_map(
        local,
        mesh=mesh,
        in_specs=placed,
        out_specs=(
            P("dp", None),
            P("dp", None),
            P(),
            P(None, "dp", None, "tensor"),
            P(None, "dp", None, "tensor"),
            P(None, "dp", None, "tensor"),
            P(None, "dp", "tensor"),
            P(None, "dp", "tensor"),
            P(None, "dp", "tensor"),
            P(None, "dp", "tensor"),
            P(None, "dp", "tensor"),
            P(None, "dp", "tensor"),
            P(None, "dp", "tensor"),
            P(None, "dp", "tensor"),
            P(None, "dp", "tensor"),
            P(),
            P(),
            P(),
        ),
        check_vma=False,
    )
```

profile of v0, /device:TPU:0, one launch (start us, length us, event | category | flops | bytes accessed | tf_op | source)
XLA Modules:
  0.0 1741.2 jit_solution(10675762374318251473)
XLA Ops:
  13.1 72.2 %all-gather.5.cloned.1.call-done = bf16[2,768,3,384]{3,1,2,0:T(8,128)(2,1)} async-done(((bf16[2,48,3,384]{3,1,2,0:T(8,128)(2,1)}), bf16[2,768,3,384]{3,1,2,0:T(8,128)(2,1)}) %all-gather.5.cloned.1.call-update) | async-done | bytes 3538960 | tf_op jit(solution)/shard_map/all_gather | solution.py:137
  85.3 5.6 fusion.209
  103.5 11.4 while.54
  116.8 26.5 %all-gather.7.cloned.1.call-done = bf16[2,768,384]{2,1,0:T(8,128)(2,1)} async-done(((bf16[2,48,384]{2,1,0:T(8,128)(2,1)}), bf16[2,768,384]{2,1,0:T(8,128)(2,1)}) %all-gather.7.cloned.1.call-update) | async-done | bytes 1179664 | tf_op jit(solution)/shard_map/all_gather | solution.py:138
  143.3 3.6 convolution_convert_fusion.1
  150.6 15.8 all-reduce.13.cloned.1.call-done
  169.4 82.1 %all-gather.9.cloned.1.call-done = bf16[2,768,1536]{2,1,0:T(8,128)(2,1)} async-done(((bf16[2,48,1536]{2,1,0:T(8,128)(2,1)}), bf16[2,768,1536]{2,1,0:T(8,128)(2,1)}) %all-gather.9.cloned.1.call-update) | async-done | bytes 4718608 | tf_op jit(solution)/shard_map/all_gather | solution.py:139
  251.5 20.8 %multiply_convert_fusion.1 = (bf16[1024,1536]{1,0:T(8,128)(2,1)}, f32[1024,1536]{1,0:T(8,128)}, f32[1024,1536]{1,0:T(8,128)}) fusion(f32[1536]{0:T(1024)S(1)} %dynamic-slice_reduce_fusion.5, bf16[2,768,1536]{2,1,0:T(8,128)(2,1)} %all-gather.9.cloned.1.call-done, f32[768]{0:T(1024)S(1)} %get-tuple-element.431, f32[768]{0:T(1024)S(1)} %get-tuple-element.432, ...), kind=kOutput, calls=%fused_computation.155 | convolution fusion | flops 2526806016 | bytes 21257216 | tf_op jit(solution)/shard_map/td,df->tf/dot_general | solution.py:190
  272.3 61.6 %all-gather.11.cloned.1.call-done = bf16[2,768,1536]{2,1,0:T(8,128)(2,1)} async-done(((bf16[2,48,1536]{2,1,0:T(8,128)(2,1)}), bf16[2,768,1536]{2,1,0:T(8,128)(2,1)}) %all-gather.11.cloned.1.call-update) | async-done | bytes 4718608 | tf_op jit(solution)/shard_map/all_gather | solution.py:140
  333.9 6.4 fusion.151
  340.5 19.1 %all-reduce.15.cloned.1.call-done = bf16[1024,768]{1,0:T(8,128)(2,1)} async-done(((bf16[1024,768]{1,0:T(8,128)(2,1)}), bf16[1024,768]{1,0:T(8,128)(2,1)}) %all-reduce.15.cloned.1.call-update) | async-done | bytes 1572880 | tf_op jit(solution)/shard_map/psum | solution.py:194
  359.6 3.6 fusion.200
  363.7 3.8 fusion.210
  380.8 14.3 while.55
  382.3 2.8 fusion.280
  389.2 2.8 fusion.280
  400.4 21.7 %all-reduce.17.cloned.1.call-done = bf16[1024,768]{1,0:T(8,128)(2,1)} async-done(((bf16[1024,768]{1,0:T(8,128)(2,1)}), bf16[1024,768]{1,0:T(8,128)(2,1)}) %all-reduce.17.cloned.1.call-update) | async-done | bytes 1572880 | tf_op jit(solution)/shard_map/psum | solution.py:181
  422.1 3.6 fusion.199
  426.5 18.6 %multiply_convert_fusion = (bf16[1024,1536]{1,0:T(8,128)(2,1)S(1)}, f32[1024,1536]{1,0:T(8,128)}, f32[1024,1536]{1,0:T(8,128)}) fusion(f32[1536]{0:T(1024)S(1)} %dynamic-slice_reduce_fusion.4, bf16[2,768,1536]{2,1,0:T(8,128)(2,1)S(1)} %bitcast.417, f32[1024,768]{1,0:T(8,128)S(1)} %get-tuple-element.545, f32[768]{0:T(1024)S(1)} %copy-done.104, ...), kind=kOutput, calls=%fused_computation.142 | convolution fusion | flops 2523660288 | bytes 21258240 | tf_op jit(solution)/shard_map/td,df->tf/dot_general | solution.py:190
  446.8 5.4 fusion.149
  452.2 21.7 %all-reduce.19.cloned.1.call-done = bf16[1024,768]{1,0:T(8,128)(2,1)} async-done(((bf16[1024,768]{1,0:T(8,128)(2,1)}), bf16[1024,768]{1,0:T(8,128)(2,1)}) %all-reduce.19.cloned.1.call-update) | async-done | bytes 1572880 | tf_op jit(solution)/shard_map/psum | solution.py:194
  473.9 3.6 fusion.197
  481.4 2.9 fusion.196
  484.4 9.5 fusion.211
  495.6 3.7 fusion.150
  503.6 8.0 convolution_bitcast_fusion.2
  511.6 9.5 all-reduce.21.cloned.1.call-done
  521.1 4.9 multiply_reduce_fusion.3
  534.4 3.3 reshape.326
  541.2 36.4 %while.56 = (s32[]{:T(128)}, bf16[2,512,6,64]{1,3,2,0:T(8,128)(2,1)}, bf16[2,512,6,64]{1,3,2,0:T(8,128)(2,1)}, f32[2,512,6,64]{1,3,2,0:T(8,128)}, f32[2,6,512,51...) while((s32[]{:T(128)}, ...), condition=%wide.region_27.28_spmd, body=%wide.region_25.27_spmd.sunk | while | flops 1227224064 | bytes 94064864 | solution.py:276
  544.8 3.4 multiply_reduce_fusion.28
  548.1 4.2 bitcast_dynamic-update-slice_fusion.8
  562.7 3.4 multiply_reduce_fusion.28
  566.1 4.3 bitcast_dynamic-update-slice_fusion.8
  577.6 2.7 fusion.206
  586.7 2.7 stack_reshape.24
  592.2 5.6 bitcast_convert_fusion.1
  598.0 7.9 convolution_bitcast_fusion
  608.8 4.3 convolution_bitcast_fusion.4
  613.1 6.5 all-reduce.23.cloned.1.call-done
  619.7 5.1 multiply_reduce_fusion.4
  627.1 9.6 fusion.212
  638.3 3.7 fusion.152
  642.1 5.6 convolution_bitcast_fusion.1
  647.8 7.4 pad_maximum_fusion.1
  655.3 4.9 convolution_bitcast_fusion.3
  660.3 3.5 all-reduce.25.cloned.1.call-done
  663.8 4.8 multiply_reduce_fusion.5
  676.7 54.2 %while.57 = (s32[]{:T(128)}, bf16[2,512,6,64]{1,3,2,0:T(8,128)(2,1)}, bf16[2,512,6,64]{1,3,2,0:T(8,128)(2,1)}, f32[2,512,6,64]{1,3,2,0:T(8,128)}, bf16[2,512,6,6...) while((s32[]{:T(128)}, ...), condition=%wide.region_36.37_spmd, body=%wide.region_34.36_spmd.sunk | while | flops 1222512128 | bytes 87736576 | solution.py:276
  676.7 5.2 exponential_select_fusion.3
  681.9 7.6 fusion.310
  689.5 7.8 fusion.311
  703.8 5.2 exponential_select_fusion.3
  709.0 7.6 fusion.310
  716.6 7.8 fusion.311
  739.8 5.2 bitcast_convert_fusion
  745.3 8.5 pad_maximum_fusion
  760.5 3.3 pad_maximum_fusion.2
  767.6 3.6 add_reduce_fusion
  772.1 736.8 %all-reduce.31.cloned.1.call-done = (f32[2,768,3,384]{3,1,2,0:T(8,128)}, f32[2,768,384]{2,1,0:T(8,128)}, f32[2,768,1536]{2,1,0:T(8,128)}, f32[2,768,1536]{2,1,0:T(8,128)}) async-done(((f32[2,768,3,384]{3,1,2,0:T(8,128)}, f32[2,768,384]{2,1,0:T(8,128)}, f32[2,768,1536]{2,1,0:T(8,128)}, f32[2,768,1536]{2,1,0:T(8,128)}), (f32[2,768,3,384]{3,1,2,0:T(8,128)}, f32[2,768,384]{2,1,0:T(8,128)}, ...) | async-done | bytes 28311568 | tf_op jit(solution)/shard_map/psum | solution.py:323
  1518.5 114.0 %all-reduce.29.cloned.1.call-done = f32[2,8448]{1,0:T(2,128)} async-done(((f32[2,8448]{1,0:T(2,128)}), f32[2,8448]{1,0:T(2,128)}) %all-reduce.29.cloned.1.call-update) | async-done | bytes 67600 | tf_op jit(solution)/shard_map/psum | solution.py:337
  1634.1 42.6 %psum.124 = f32[]{:T(128)} all-reduce(f32[]{:T(128)S(6)} %add.424), channel_id=1, replica_groups=mesh['dp'=16,'tensor'=2] {'dp','tensor'}, use_global_device_ids=true, to_apply=%region_46.47 | all-reduce | flops 1 | bytes 8 | tf_op jit(solution)/shard_map/psum | solution.py:337
  1682.0 3.2 multiply_reduce_fusion.16
  1687.8 39.3 %all-reduce = (f32[4,2]{1,0:T(4,128)S(1)}, f32[4,2]{1,0:T(4,128)S(1)}) all-reduce(f32[4,2]{1,0:T(4,128)S(1)} %pad_maximum_fusion.12, f32[4,2]{1,0:T(4,128)S(1)} %pad_maximum_fusion.11), channel_id=1, replica_groups=mesh['dp'=16,'tensor'=2] {'dp','tensor'}, use_global_device_ids=true, to_apply=%region_74.75 | all-reduce | flops 16 | bytes 128 | tf_op jit(solution)/shard_map/psum | solution.py:353
  (526 shorter events, 188.6 us)
Async XLA Ops:
  7.2 78.1 %all-gather.5.cloned.1.call-start = ((), (), s32[]{:S(2)}) async-start(), calls=%async_computation | async-start | bytes 3760128 | tf_op jit(solution)/shard_map/all_gather | solution.py:137
  9.0 134.3 %all-gather.7.cloned.1.call-start = ((), (), s32[]{:S(2)}) async-start(), calls=%async_computation.1 | async-start | bytes 1253376 | tf_op jit(solution)/shard_map/all_gather | solution.py:138
  10.6 155.7 %all-reduce.13.cloned.1.call-start = ((), (), s32[]{:S(2)}) async-start(), calls=%async_computation.2 | async-start | bytes 3145728 | tf_op jit(solution)/shard_map/psum | solution.py:181
  12.2 347.3 %copy-start.73 = (f32[768]{0:T(1024)}, f32[768]{0:T(1024)S(1)}, u32[]{:S(2)}) copy-start(f32[768]{0:T(1024)S(1)} %get-tuple-element.433) | copy-start | bytes 9220
  12.2 347.3 %copy-start.82 = (f32[768]{0:T(1024)}, f32[768]{0:T(1024)S(1)}, u32[]{:S(2)}) copy-start(f32[768]{0:T(1024)S(1)} %get-tuple-element.432) | copy-start | bytes 9220
  12.2 347.3 %copy-start.100 = (f32[768]{0:T(1024)}, f32[768]{0:T(1024)S(1)}, u32[]{:S(2)}) copy-start(f32[768]{0:T(1024)S(1)} %get-tuple-element.431) | copy-start | bytes 9220
  12.2 409.8 %copy-start.86 = (f32[768]{0:T(1024)}, f32[768]{0:T(1024)S(1)}, u32[]{:S(2)}) copy-start(f32[768]{0:T(1024)S(1)} %get-tuple-element.429) | copy-start | bytes 9220
  12.2 409.8 %copy-start.102 = (f32[768]{0:T(1024)}, f32[768]{0:T(1024)S(1)}, u32[]{:S(2)}) copy-start(f32[768]{0:T(1024)S(1)} %get-tuple-element.428) | copy-start | bytes 9220
  114.9 28.3 %copy-start.20 = (bf16[2,512,6,64]{1,3,2,0:T(8,128)(2,1)}, bf16[2,512,6,64]{1,3,2,0:T(8,128)(2,1)S(1)}, u32[]{:S(2)}) copy-start(bf16[2,512,6,64]{1,3,2,0:T(8,128)(2,1)S(1)} %get-tuple-element.1014) | copy-start | bytes 2359300
  114.9 31.9 %copy-start.69 = (f32[2,6,512]{2,1,0:T(8,128)}, f32[2,6,512]{2,1,0:T(8,128)S(1)}, u32[]{:S(2)}) copy-start(f32[2,6,512]{2,1,0:T(8,128)S(1)} %get-tuple-element.954) | copy-start | bytes 73732
  116.8 32.0 %copy-start.32 = (f32[2,48,1536]{2,1,0:T(8,128)S(1)}, f32[2,48,1536]{2,1,0:T(8,128)}, u32[]{:S(2)}) copy-start(f32[2,48,1536]{2,1,0:T(8,128)} %param.32) | copy-start | bytes 1769476
  143.3 23.1 %copy-start.10 = (bf16[1024,768]{1,0:T(8,128)(2,1)S(1)}, bf16[1024,768]{1,0:T(8,128)(2,1)}, u32[]{:S(2)}) copy-start(bf16[1024,768]{1,0:T(8,128)(2,1)} %param.26) | copy-start | bytes 4718596
  146.9 104.6 %all-gather.9.cloned.1.call-start = ((), (), s32[]{:S(2)}) async-start(), calls=%async_computation.3 | async-start | bytes 5013504 | tf_op jit(solution)/shard_map/all_gather | solution.py:139
  148.8 185.2 %all-gather.11.cloned.1.call-start = ((), (), s32[]{:S(2)}) async-start(), calls=%async_computation.4 | async-start | bytes 5013504 | tf_op jit(solution)/shard_map/all_gather | solution.py:140
  149.6 209.9 %all-reduce.15.cloned.1.call-start = ((), (), s32[]{:S(2)}) async-start(), calls=%async_computation.5 | async-start | bytes 3145728 | tf_op jit(solution)/shard_map/psum | solution.py:194
  150.5 100.9 %copy-start.116 = (f32[1536]{0:T(1024)}, f32[1536]{0:T(1024)S(1)}, u32[]{:S(2)}) copy-start(f32[1536]{0:T(1024)S(1)} %dynamic-slice_reduce_fusion.5) | copy-start | bytes 18436
  168.5 191.1 %copy-start.76 = (f32[1024]{0:T(1024)}, f32[1024]{0:T(1024)S(1)}, u32[]{:S(2)}) copy-start(f32[1024]{0:T(1024)S(1)} %broadcast_multiply_fusion.3) | copy-start | bytes 12292
  169.4 102.9 %copy-start.92 = (f32[1024]{0:T(1024)}, f32[1024]{0:T(1024)S(1)}, u32[]{:S(2)}) copy-start(f32[1024]{0:T(1024)S(1)} %multiply_reduce_fusion.13) | copy-start | bytes 12292
  169.4 190.2 %copy-start.84 = (f32[1024]{0:T(1024)}, f32[1024]{0:T(1024)S(1)}, u32[]{:S(2)}) copy-start(f32[1024]{0:T(1024)S(1)} %fusion.167) | copy-start | bytes 12292
  340.4 81.7 %all-reduce.17.cloned.1.call-start = ((), (), s32[]{:S(2)}) async-start(), calls=%async_computation.6 | async-start | bytes 3145728 | tf_op jit(solution)/shard_map/psum | solution.py:181
  363.2 58.9 %copy-start.78 = (f32[1024]{0:T(1024)}, f32[1024]{0:T(1024)S(1)}, u32[]{:S(2)}) copy-start(f32[1024]{0:T(1024)S(1)} %broadcast_multiply_fusion.2) | copy-start | bytes 12292
  363.7 58.4 %copy-start.89 = (f32[1024]{0:T(1024)}, f32[1024]{0:T(1024)S(1)}, u32[]{:S(2)}) copy-start(f32[1024]{0:T(1024)S(1)} %fusion.168) | copy-start | bytes 12292
  397.1 25.0 %copy-start.106 = (f32[768]{0:T(1024)S(1)}, f32[768]{0:T(1024)}, u32[]{:S(2)}) copy-start(f32[768]{0:T(1024)} %get-tuple-element.427) | copy-start | bytes 9220
  400.3 73.6 %all-reduce.19.cloned.1.call-start = ((), (), s32[]{:S(2)}) async-start(), calls=%async_computation.7 | async-start | bytes 3145728 | tf_op jit(solution)/shard_map/psum | solution.py:194
  425.8 19.4 %copy-start.3 = (f32[1024,768]{1,0:T(8,128)}, f32[1024,768]{1,0:T(8,128)S(1)}, u32[]{:S(2)}) copy-start(f32[1024,768]{1,0:T(8,128)S(1)} %get-tuple-element.545) | copy-start | bytes 9437188
  446.8 27.2 %copy-start.105 = (f32[768]{0:T(1024)S(1)}, f32[768]{0:T(1024)}, u32[]{:S(2)}) copy-start(f32[768]{0:T(1024)} %get-tuple-element.424) | copy-start | bytes 9220
  452.2 68.9 %all-reduce.21.cloned.1.call-start = ((), (), s32[]{:S(2)}) async-start(), calls=%async_computation.8 | async-start | bytes 3145728 | tf_op jit(solution)/shard_map/psum | solution.py:246
  473.9 10.4 slice-start.8
  481.4 14.2 slice-start.4
  484.4 9.6 copy-start.8
  484.4 11.2 slice-start.5
  499.3 120.3 %all-reduce.23.cloned.1.call-start = ((), (), s32[]{:S(2)}) async-start(), calls=%async_computation.9 | async-start | bytes 3145728 | tf_op jit(solution)/shard_map/psum | solution.py:293
  582.6 7.9 copy-start.40
  597.9 7.9 copy-start.53
  597.9 65.9 %all-reduce.25.cloned.1.call-start = ((), (), s32[]{:S(2)}) async-start(), calls=%async_computation.10 | async-start | bytes 3145728 | tf_op jit(solution)/shard_map/psum | solution.py:246
  598.0 7.9 copy-start.18
  598.0 10.3 copy-start.63
  613.1 11.7 copy-start.95
  625.2 13.1 slice-start.6
  627.1 9.6 copy-start.6
  627.1 11.3 slice-start.7
  642.1 125.4 %all-reduce.27.cloned.1.call-start = ((), (), s32[]{:S(2)}) async-start(), calls=%async_computation.11 | async-start | bytes 3145728 | tf_op jit(solution)/shard_map/psum | solution.py:293
  647.8 7.5 copy-start.11
  647.8 7.5 copy-start.14
  647.8 7.5 copy-start.74
  647.8 7.5 copy-start.77
  647.8 7.5 copy-start.83
  660.3 8.4 copy-start.93
  681.9 19.8 %slice-start = ((s8[6291456]{0:T(1024)(128)(4,1)}), s8[2097152]{0:T(1024)(128)(4,1)S(1)}, s32[]{:S(2)}) async-start(s8[6291456]{0:T(1024)(128)(4,1)} %bitcast.400), calls=%async_computation.14 | async-start | bytes 4194304 | tf_op jit(solution)/shard_map/while
  689.5 12.2 slice-start.1
  709.0 19.8 %slice-start = ((s8[6291456]{0:T(1024)(128)(4,1)}), s8[2097152]{0:T(1024)(128)(4,1)S(1)}, s32[]{:S(2)}) async-start(s8[6291456]{0:T(1024)(128)(4,1)} %bitcast.400), calls=%async_computation.14 | async-start | bytes 4194304 | tf_op jit(solution)/shard_map/while
  716.6 12.2 slice-start.1
  736.6 8.4 copy-start.57
  745.0 8.8 copy-start.26
  745.0 763.9 %all-reduce.31.cloned.1.call-start = ((), (), s32[]{:S(2)}) async-start(), calls=%async_computation.13 | async-start | bytes 56623104 | tf_op jit(solution)/shard_map/psum | solution.py:323
  745.3 8.5 copy-start.51
  763.9 868.6 %all-reduce.29.cloned.1.call-start = ((), (), s32[]{:S(2)}) async-start(), calls=%async_computation.12 | async-start | bytes 135168 | tf_op jit(solution)/shard_map/psum | solution.py:337
  767.5 910.6 %copy-start.47 = (f32[2,48,384]{2,1,0:T(8,128)S(1)}, f32[2,48,384]{2,1,0:T(8,128)}, u32[]{:S(2)}) copy-start(f32[2,48,384]{2,1,0:T(8,128)} %param.30) | copy-start | bytes 442372
  771.2 908.8 %copy-start.34 = (f32[2,48,1536]{2,1,0:T(8,128)S(1)}, f32[2,48,1536]{2,1,0:T(8,128)}, u32[]{:S(2)}) copy-start(f32[2,48,1536]{2,1,0:T(8,128)} %param.31) | copy-start | bytes 1769476
  771.2 908.8 %copy-start.66 = (f32[2,48,1536]{2,1,0:T(8,128)S(1)}, f32[2,48,1536]{2,1,0:T(8,128)}, u32[]{:S(2)}) copy-start(f32[2,48,1536]{2,1,0:T(8,128)} %param.38) | copy-start | bytes 1769476
  1508.9 173.1 %copy-start.33 = (f32[2,48,1536]{2,1,0:T(8,128)S(1)}, f32[2,48,1536]{2,1,0:T(8,128)}, u32[]{:S(2)}) copy-start(f32[2,48,1536]{2,1,0:T(8,128)} %param.32) | copy-start | bytes 1769476
  1682.0 47.4 %copy-start.42 = (f32[2,48,1536]{2,1,0:T(8,128)}, f32[2,48,1536]{2,1,0:T(8,128)S(1)}, u32[]{:S(2)}) copy-start(f32[2,48,1536]{2,1,0:T(8,128)S(1)} %get-tuple-element.528) | copy-start | bytes 1769476
  1682.0 47.4 %copy-start.43 = (f32[2,48,1536]{2,1,0:T(8,128)}, f32[2,48,1536]{2,1,0:T(8,128)S(1)}, u32[]{:S(2)}) copy-start(f32[2,48,1536]{2,1,0:T(8,128)S(1)} %get-tuple-element.529) | copy-start | bytes 1769476
  1685.2 45.4 %copy-start.44 = (f32[2,48,1536]{2,1,0:T(8,128)}, f32[2,48,1536]{2,1,0:T(8,128)S(1)}, u32[]{:S(2)}) copy-start(f32[2,48,1536]{2,1,0:T(8,128)S(1)} %get-tuple-element.530) | copy-start | bytes 1769476
  (95 other events, 299.0 us)
Sparse Core Ops, SparseCore 0:
  11.3 73.9 all-gather.4
  88.5 54.6 all-gather.6
  147.0 19.2 all-reduce.12
  169.8 81.6 all-gather.8
  255.0 78.9 all-gather.10
  340.5 19.0 all-reduce.14
  400.5 21.5 all-reduce.16
  452.3 21.5 all-reduce.18
  499.5 21.5 all-reduce.20
  598.0 21.5 all-reduce.22
  642.2 21.5 all-reduce.24
  745.1 21.5 all-reduce.26
  773.2 735.7 all-reduce.30
  1515.9 116.6 all-reduce.28
where the time goes:
time: 1750 us; the launch traced here: 1740 us
  waiting for transfers between devices  1190 us (68%)
  matrix products  238 us (14%)
  other arithmetic  120 us (7%)
  local copies, waits for them, and re-layouts  86.9 us (5%)
  blocking collectives  81.9 us (5%)
  between operations  20.9 us (1%)
    psum x1, waiting for transfers between devices, local(): lax.psum((big_totals[0], big_totals[1], big_totals[2], big_totals[3]), 'dp')  737 us
    psum x1, waiting for transfers between devices, local(): lax.psum((square_part, weight_square, small_partial), ('dp', 'tensor'))  114 us
    all_gather x1, waiting for transfers between devices, local(): lax.all_gather(up_weight.astype(jnp.bfloat16), 'dp', axis=1, tiled=True)  82.1 us
    all_gather x1, waiting for transfers between devices, local(): lax.all_gather(proj_weight.astype(jnp.bfloat16), 'dp', axis=1, tiled=True)  72.2 us
    all_gather x1, waiting for transfers between devices, local(): lax.all_gather(down_weight.astype(jnp.bfloat16), 'dp', axis=1, tiled=True)  61.6 us
    psum x1, blocking collectives, local(): lax.psum((square_part, weight_square, small_partial), ('dp', 'tensor'))  42.6 us
    psum x2, waiting for transfers between devices, local(): lax.psum(jnp.einsum('tf,df->td', act_low, down_full[layer_at], preferred_...  40.7 us
    dot_general x2, matrix products, local(): jnp.einsum('td,df->tf', first_low, up_full[layer_at], preferred_element_t...  39.4 us
  transfers between devices with their start and end apart: 14, of which 13 were waited for; matrix products, arithmetic and copies ran while one was open for 8% of the time, Pallas kernels for 0%

commit v1 on v0

--- a/solution.py
+++ b/solution.py
@@ -18,6 +18,11 @@
 step_count = 10.0
 norm_eps = 1e-06
 masked_score = -1e30
+
+
+def gather_over(shard, name, dim):
+    sent = jnp.stack([shard] * lax.axis_size(name))
+    return jnp.concatenate(lax.all_to_all(sent, name, 0, 0), axis=dim)
 
 
 def layer_norm(values, norm_gain, norm_shift):
@@ -137,7 +142,7 @@
         lax.all_gather(proj_weight.astype(jnp.bfloat16), "dp", axis=1, tiled=True),
         lax.all_gather(out_weight.astype(jnp.bfloat16), "dp", axis=1, tiled=True),
         lax.all_gather(up_weight.astype(jnp.bfloat16), "dp", axis=1, tiled=True),
-        lax.all_gather(down_weight.astype(jnp.bfloat16), "dp", axis=1, tiled=True),
+        gather_over(down_weight.astype(jnp.bfloat16), "dp", 1),
     )
     positions = jnp.arange(seq_len)
     key_valid = positions[None, :] < lengths[:, None]

time: 1750 us -> 1730 us (0.989)
    all_to_all x0 -> x1, waiting for transfers between devices: none -> 91.1 us  [gather_over(): return jnp.concatenate(lax.all_to_all(sent, name, 0, 0), axis=dim)]
    all_gather x1 -> x0, waiting for transfers between devices: 61.6 us -> none  [local(): lax.all_gather(down_weight.astype(jnp.bfloat16), 'dp', axis=1, tiled=True)]
    all_gather x1, waiting for transfers between devices: 82.1 us -> 36.2 us  [local(): lax.all_gather(up_weight.astype(jnp.bfloat16), 'dp', axis=1, tiled=True)]
  transfers between devices with their start and end apart: 14 -> 14, of which waited for: 13 -> 14; matrix products, arithmetic and copies ran while one was open for 8% -> 7% of each run, Pallas kernels for 0% -> 0%
where the time goes in v1:
time: 1730 us; the launch traced here: 1720 us
  waiting for transfers between devices  1180 us (68%)
  matrix products  230 us (13%)
  other arithmetic  120 us (7%)
  blocking collectives  81.9 us (5%)
  local copies, waits for them, and re-layouts  80.6 us (5%)
  between operations  21 us (1%)
    psum x1, waiting for transfers between devices, local(): lax.psum((big_totals[0], big_totals[1], big_totals[2], big_totals[3]), 'dp')  737 us
    psum x1, waiting for transfers between devices, local(): lax.psum((square_part, weight_square, small_partial), ('dp', 'tensor'))  114 us
    all_to_all x1, waiting for transfers between devices, gather_over(): return jnp.concatenate(lax.all_to_all(sent, name, 0, 0), axis=dim)  91.1 us
    all_gather x1, waiting for transfers between devices, local(): lax.all_gather(proj_weight.astype(jnp.bfloat16), 'dp', axis=1, tiled=True)  72.2 us
    psum x2, waiting for transfers between devices, local(): lax.psum(jnp.einsum('tf,df->td', act_low, down_full[layer_at], preferred_...  45.5 us
    psum x1, blocking collectives, local(): lax.psum((square_part, weight_square, small_partial), ('dp', 'tensor'))  42.6 us
    psum x1, blocking collectives, local(): update_square = lax.psum(update_square, ('dp', 'tensor'))  39.3 us
    dot_general x2, matrix products, local(): jnp.einsum('td,df->tf', first_low, up_full[layer_at], preferred_element_t...  39.2 us
  transfers between devices with their start and end apart: 14, of which 14 were waited for; matrix products, arithmetic and copies ran while one was open for 7% of the time, Pallas kernels for 0%

profile of v1, /device:TPU:0, one launch (start us, length us, event | category | flops | bytes accessed | tf_op | source)
XLA Modules:
  0.0 1721.5 jit_solution(15477596357881578237)
XLA Ops:
  13.1 72.2 %all-gather.4.cloned.1.call-done = bf16[2,768,3,384]{3,1,2,0:T(8,128)(2,1)} async-done(((bf16[2,48,3,384]{3,1,2,0:T(8,128)(2,1)}), bf16[2,768,3,384]{3,1,2,0:T(8,128)(2,1)}) %all-gather.4.cloned.1.call-update) | async-done | bytes 3538960 | tf_op jit(solution)/shard_map/all_gather | solution.py:142
  85.3 5.6 fusion.206
  92.6 2.8 squeeze.116
  100.1 11.4 while.54
  112.5 30.8 %all-gather.6.cloned.1.call-done = bf16[2,768,384]{2,1,0:T(8,128)(2,1)} async-done(((bf16[2,48,384]{2,1,0:T(8,128)(2,1)}), bf16[2,768,384]{2,1,0:T(8,128)(2,1)}) %all-gather.6.cloned.1.call-update) | async-done | bytes 1179664 | tf_op jit(solution)/shard_map/all_gather | solution.py:143
  143.3 3.2 convolution_convert_fusion.1
  149.3 4.7 all-to-all-start
  156.0 10.0 all-reduce.13.cloned.1.call-done
  169.0 91.1 %all-to-all-done = bf16[16,2,48,1536]{3,2,1,0:T(8,128)(2,1)} async-done(((bf16[16,2,48,1536]{3,2,1,0:T(8,128)(2,1)}), bf16[16,2,48,1536]{3,2,1,0:T(8,128)(2,1)}, u32[]{:S(2)}, u32[]{:S(2)}) %all-to-all-start) | async-done | bytes 4718624 | tf_op jit(solution)/shard_map/all_to_all | solution.py:25
  260.2 5.5 fusion.199
  265.7 36.2 %all-gather.8.cloned.1.call-done = bf16[2,768,1536]{2,1,0:T(8,128)(2,1)} async-done(((bf16[2,48,1536]{2,1,0:T(8,128)(2,1)}), bf16[2,768,1536]{2,1,0:T(8,128)(2,1)}) %all-gather.8.cloned.1.call-update) | async-done | bytes 4718608 | tf_op jit(solution)/shard_map/all_gather | solution.py:144
  301.9 20.5 %multiply_convert_fusion.1 = (bf16[1024,1536]{1,0:T(8,128)(2,1)S(1)}, f32[1024,1536]{1,0:T(8,128)}, f32[1024,1536]{1,0:T(8,128)}) fusion(f32[1536]{0:T(1024)S(1)} %dynamic-slice_reduce_fusion.5, bf16[2,768,1536]{2,1,0:T(8,128)(2,1)} %all-gather.8.cloned.1.call-done, f32[768]{0:T(1024)S(1)} %get-tuple-element.431, f32[768]{0:T(1024)S(1)} %get-tuple-element.432, ...), kind=kOutput, calls=%fused_computation.155 | convolution fusion | flops 2526806016 | bytes 21257216 | tf_op jit(solution)/shard_map/td,df->tf/dot_general | solution.py:195
  324.1 3.7 convolution_convert_fusion.3
  328.4 23.8 %all-reduce.15.cloned.1.call-done = bf16[1024,768]{1,0:T(8,128)(2,1)} async-done(((bf16[1024,768]{1,0:T(8,128)(2,1)}), bf16[1024,768]{1,0:T(8,128)(2,1)}) %all-reduce.15.cloned.1.call-update) | async-done | bytes 1572880 | tf_op jit(solution)/shard_map/psum | solution.py:199
  352.3 3.3 fusion.196
  356.1 3.8 fusion.207
  373.1 13.5 while.55
  374.3 2.8 fusion.281
  381.0 2.8 fusion.281
  392.3 21.6 %all-reduce.17.cloned.1.call-done = bf16[1024,768]{1,0:T(8,128)(2,1)} async-done(((bf16[1024,768]{1,0:T(8,128)(2,1)}), bf16[1024,768]{1,0:T(8,128)(2,1)}) %all-reduce.17.cloned.1.call-update) | async-done | bytes 1572880 | tf_op jit(solution)/shard_map/psum | solution.py:186
  413.9 3.6 fusion.195
  418.4 18.7 %multiply_convert_fusion = (bf16[1024,1536]{1,0:T(8,128)(2,1)S(1)}, f32[1024,1536]{1,0:T(8,128)}, f32[1024,1536]{1,0:T(8,128)}) fusion(f32[1536]{0:T(1024)S(1)} %dynamic-slice_reduce_fusion.4, bf16[2,768,1536]{2,1,0:T(8,128)(2,1)S(1)} %bitcast.408, f32[1024,768]{1,0:T(8,128)S(1)} %get-tuple-element.545, f32[768]{0:T(1024)S(1)} %copy-done.100, ...), kind=kOutput, calls=%fused_computation.142 | convolution fusion | flops 2523660288 | bytes 21258240 | tf_op jit(solution)/shard_map/td,df->tf/dot_general | solution.py:195
  438.7 3.7 convolution_convert_fusion.2
  442.5 21.7 %all-reduce.19.cloned.1.call-done = bf16[1024,768]{1,0:T(8,128)(2,1)} async-done(((bf16[1024,768]{1,0:T(8,128)(2,1)}), bf16[1024,768]{1,0:T(8,128)(2,1)}) %all-reduce.19.cloned.1.call-update) | async-done | bytes 1572880 | tf_op jit(solution)/shard_map/psum | solution.py:199
  464.1 3.6 fusion.193
  471.9 2.9 fusion.192
  474.9 8.6 fusion.208
  485.1 3.8 fusion.145
  491.7 8.0 convolution_bitcast_fusion.2
  499.7 10.9 all-reduce.21.cloned.1.call-done
  510.6 4.9 multiply_reduce_fusion.3
  527.1 36.1 %while.56 = (s32[]{:T(128)}, bf16[2,512,6,64]{1,3,2,0:T(8,128)(2,1)}, bf16[2,512,6,64]{1,3,2,0:T(8,128)(2,1)}, f32[2,512,6,64]{1,3,2,0:T(8,128)}, f32[2,6,512,51...) while((s32[]{:T(128)}, ...), condition=%wide.region_27.28_spmd, body=%wide.region_25.27_spmd.sunk | while | flops 1227224064 | bytes 90919112 | solution.py:281
  530.4 3.3 multiply_reduce_fusion.28
  533.7 4.3 bitcast_dynamic-update-slice_fusion.8
  548.3 3.4 multiply_reduce_fusion.28
  551.6 4.3 bitcast_dynamic-update-slice_fusion.8
  572.8 5.3 bitcast_convert_fusion.1
  578.7 7.8 convolution_bitcast_fusion
  589.5 4.4 convolution_bitcast_fusion.4
  593.9 6.0 all-reduce.23.cloned.1.call-done
  599.9 4.9 multiply_reduce_fusion.4
  607.4 8.9 fusion.209
  618.0 3.7 fusion.146
  621.8 5.6 convolution_bitcast_fusion.1
  627.5 7.4 pad_maximum_fusion.1
  635.0 4.8 convolution_bitcast_fusion.3
  639.8 3.7 all-reduce.25.cloned.1.call-done
  643.5 4.2 multiply_reduce_fusion.5
  656.2 54.4 %while.57 = (s32[]{:T(128)}, bf16[2,512,6,64]{1,3,2,0:T(8,128)(2,1)}, bf16[2,512,6,64]{1,3,2,0:T(8,128)(2,1)}, f32[2,512,6,64]{1,3,2,0:T(8,128)}, bf16[2,512,6,6...) while((s32[]{:T(128)}, ...), condition=%wide.region_36.37_spmd, body=%wide.region_34.36_spmd.sunk | while | flops 1222512128 | bytes 87736576 | solution.py:281
  656.2 5.2 exponential_select_fusion.3
  661.4 7.6 fusion.311
  669.0 7.8 fusion.312
  683.3 5.2 exponential_select_fusion.3
  688.5 7.6 fusion.311
  696.1 7.8 fusion.312
  719.1 5.2 bitcast_convert_fusion
  724.7 8.5 pad_maximum_fusion
  739.4 3.4 pad_maximum_fusion.2
  746.1 4.5 add_reduce_fusion
  751.4 736.7 %all-reduce.31.cloned.1.call-done = (f32[2,768,3,384]{3,1,2,0:T(8,128)}, f32[2,768,384]{2,1,0:T(8,128)}, f32[2,768,1536]{2,1,0:T(8,128)}, f32[2,768,1536]{2,1,0:T(8,128)}) async-done(((f32[2,768,3,384]{3,1,2,0:T(8,128)}, f32[2,768,384]{2,1,0:T(8,128)}, f32[2,768,1536]{2,1,0:T(8,128)}, f32[2,768,1536]{2,1,0:T(8,128)}), (f32[2,768,3,384]{3,1,2,0:T(8,128)}, f32[2,768,384]{2,1,0:T(8,128)}, ...) | async-done | bytes 28311568 | tf_op jit(solution)/shard_map/psum | solution.py:328
  1497.7 114.2 %all-reduce.29.cloned.1.call-done = f32[2,8448]{1,0:T(2,128)} async-done(((f32[2,8448]{1,0:T(2,128)}), f32[2,8448]{1,0:T(2,128)}) %all-reduce.29.cloned.1.call-update) | async-done | bytes 67600 | tf_op jit(solution)/shard_map/psum | solution.py:342
  1613.5 42.6 %psum.124 = f32[]{:T(128)} all-reduce(f32[]{:T(128)S(6)} %add.424), channel_id=1, replica_groups=mesh['dp'=16,'tensor'=2] {'dp','tensor'}, use_global_device_ids=true, to_apply=%region_46.47 | all-reduce | flops 1 | bytes 8 | tf_op jit(solution)/shard_map/psum | solution.py:342
  1661.4 3.4 multiply_reduce_fusion.16
  1667.0 39.3 %all-reduce = (f32[4,2]{1,0:T(4,128)S(1)}, f32[4,2]{1,0:T(4,128)S(1)}) all-reduce(f32[4,2]{1,0:T(4,128)S(1)} %pad_maximum_fusion.12, f32[4,2]{1,0:T(4,128)S(1)} %pad_maximum_fusion.11), channel_id=1, replica_groups=mesh['dp'=16,'tensor'=2] {'dp','tensor'}, use_global_device_ids=true, to_apply=%region_74.75 | all-reduce | flops 16 | bytes 128 | tf_op jit(solution)/shard_map/psum | solution.py:358
  (515 shorter events, 183.6 us)
Async XLA Ops:
  7.2 78.1 %all-gather.4.cloned.1.call-start = ((), (), s32[]{:S(2)}) async-start(), calls=%async_computation.1 | async-start | bytes 3760128 | tf_op jit(solution)/shard_map/all_gather | solution.py:142
  9.0 134.3 %all-gather.6.cloned.1.call-start = ((), (), s32[]{:S(2)}) async-start(), calls=%async_computation.2 | async-start | bytes 1253376 | tf_op jit(solution)/shard_map/all_gather | solution.py:143
  10.6 155.4 %all-reduce.13.cloned.1.call-start = ((), (), s32[]{:S(2)}) async-start(), calls=%async_computation.3 | async-start | bytes 3145728 | tf_op jit(solution)/shard_map/psum | solution.py:186
  12.2 340.0 %copy-start.71 = (f32[768]{0:T(1024)}, f32[768]{0:T(1024)S(1)}, u32[]{:S(2)}) copy-start(f32[768]{0:T(1024)S(1)} %get-tuple-element.433) | copy-start | bytes 9220
  12.2 340.0 %copy-start.81 = (f32[768]{0:T(1024)}, f32[768]{0:T(1024)S(1)}, u32[]{:S(2)}) copy-start(f32[768]{0:T(1024)S(1)} %get-tuple-element.432) | copy-start | bytes 9220
  12.2 340.0 %copy-start.96 = (f32[768]{0:T(1024)}, f32[768]{0:T(1024)S(1)}, u32[]{:S(2)}) copy-start(f32[768]{0:T(1024)S(1)} %get-tuple-element.431) | copy-start | bytes 9220
  12.2 401.7 %copy-start.85 = (f32[768]{0:T(1024)}, f32[768]{0:T(1024)S(1)}, u32[]{:S(2)}) copy-start(f32[768]{0:T(1024)S(1)} %get-tuple-element.429) | copy-start | bytes 9220
  12.2 401.7 %copy-start.98 = (f32[768]{0:T(1024)}, f32[768]{0:T(1024)S(1)}, u32[]{:S(2)}) copy-start(f32[768]{0:T(1024)S(1)} %get-tuple-element.428) | copy-start | bytes 9220
  111.5 35.0 %copy-start.19 = (bf16[2,512,6,64]{1,3,2,0:T(8,128)(2,1)}, bf16[2,512,6,64]{1,3,2,0:T(8,128)(2,1)S(1)}, u32[]{:S(2)}) copy-start(bf16[2,512,6,64]{1,3,2,0:T(8,128)(2,1)S(1)} %get-tuple-element.1015) | copy-start | bytes 2359300
  112.4 34.2 %copy-start.31 = (f32[2,48,1536]{2,1,0:T(8,128)S(1)}, f32[2,48,1536]{2,1,0:T(8,128)}, u32[]{:S(2)}) copy-start(f32[2,48,1536]{2,1,0:T(8,128)} %param.32) | copy-start | bytes 1769476
  112.5 34.1 %copy-start.55 = (bf16[48,8,2,512]{3,1,2,0:T(8,128)(2,1)}, bf16[48,8,2,512]{3,1,2,0:T(8,128)(2,1)S(1)}, u32[]{:S(2)}) copy-start(bf16[48,8,2,512]{3,1,2,0:T(8,128)(2,1)S(1)} %copy.197) | copy-start | bytes 2359300
  149.3 16.7 copy-start.10
  149.3 110.9 %all-to-all-start = ((bf16[16,2,48,1536]{3,2,1,0:T(8,128)(2,1)}), bf16[16,2,48,1536]{3,2,1,0:T(8,128)(2,1)}, u32[]{:S(2)}, u32[]{:S(2)}) async-start(bf16[16,2,48,1536]{3,2,1,0:T(8,128)(2,1)} %stack.102), calls=%async_computation | async-start | bytes 9437184 | tf_op jit(solution)/shard_map/all_to_all | solution.py:25
  154.0 147.9 %all-gather.8.cloned.1.call-start = ((), (), s32[]{:S(2)}) async-start(), calls=%async_computation.4 | async-start | bytes 5013504 | tf_op jit(solution)/shard_map/all_gather | solution.py:144
  154.8 197.4 %all-reduce.15.cloned.1.call-start = ((), (), s32[]{:S(2)}) async-start(), calls=%async_computation.5 | async-start | bytes 3145728 | tf_op jit(solution)/shard_map/psum | solution.py:199
  156.0 145.9 %copy-start.112 = (f32[1536]{0:T(1024)}, f32[1536]{0:T(1024)S(1)}, u32[]{:S(2)}) copy-start(f32[1536]{0:T(1024)S(1)} %dynamic-slice_reduce_fusion.5) | copy-start | bytes 18436
  168.1 184.1 %copy-start.75 = (f32[1024]{0:T(1024)}, f32[1024]{0:T(1024)S(1)}, u32[]{:S(2)}) copy-start(f32[1024]{0:T(1024)S(1)} %broadcast_multiply_fusion.3) | copy-start | bytes 12292
  169.0 96.7 %copy-start.91 = (f32[1024]{0:T(1024)}, f32[1024]{0:T(1024)S(1)}, u32[]{:S(2)}) copy-start(f32[1024]{0:T(1024)S(1)} %multiply_reduce_fusion.13) | copy-start | bytes 12292
  169.0 183.2 %copy-start.83 = (f32[1024]{0:T(1024)}, f32[1024]{0:T(1024)S(1)}, u32[]{:S(2)}) copy-start(f32[1024]{0:T(1024)S(1)} %fusion.161) | copy-start | bytes 12292
  301.9 22.2 %copy-start.45 = (bf16[1,16,48,1536]{3,2,0,1:T(8,128)(2,1)S(1)}, bf16[1,16,48,1536]{3,2,0,1:T(8,128)(2,1)}, u32[]{:S(2)}) copy-start(bf16[1,16,48,1536]{3,2,0,1:T(8,128)(2,1)} %get-tuple-element.557) | copy-start | bytes 7077892
  327.9 86.0 %all-reduce.17.cloned.1.call-start = ((), (), s32[]{:S(2)}) async-start(), calls=%async_computation.6 | async-start | bytes 3145728 | tf_op jit(solution)/shard_map/psum | solution.py:186
  355.6 58.3 %copy-start.77 = (f32[1024]{0:T(1024)}, f32[1024]{0:T(1024)S(1)}, u32[]{:S(2)}) copy-start(f32[1024]{0:T(1024)S(1)} %broadcast_multiply_fusion.2) | copy-start | bytes 12292
  356.1 57.8 %copy-start.88 = (f32[1024]{0:T(1024)}, f32[1024]{0:T(1024)S(1)}, u32[]{:S(2)}) copy-start(f32[1024]{0:T(1024)S(1)} %fusion.162) | copy-start | bytes 12292
  388.9 25.0 %copy-start.102 = (f32[768]{0:T(1024)S(1)}, f32[768]{0:T(1024)}, u32[]{:S(2)}) copy-start(f32[768]{0:T(1024)} %get-tuple-element.427) | copy-start | bytes 9220
  392.2 72.0 %all-reduce.19.cloned.1.call-start = ((), (), s32[]{:S(2)}) async-start(), calls=%async_computation.7 | async-start | bytes 3145728 | tf_op jit(solution)/shard_map/psum | solution.py:199
  417.6 19.4 %copy-start.3 = (f32[1024,768]{1,0:T(8,128)}, f32[1024,768]{1,0:T(8,128)S(1)}, u32[]{:S(2)}) copy-start(f32[1024,768]{1,0:T(8,128)S(1)} %get-tuple-element.545) | copy-start | bytes 9437188
  418.3 20.3 %copy-start.47 = (bf16[1,16,48,1536]{3,2,0,1:T(8,128)(2,1)S(1)}, bf16[1,16,48,1536]{3,2,0,1:T(8,128)(2,1)}, u32[]{:S(2)}) copy-start(bf16[1,16,48,1536]{3,2,0,1:T(8,128)(2,1)} %get-tuple-element.556) | copy-start | bytes 7077892
  438.7 25.5 %copy-start.101 = (f32[768]{0:T(1024)S(1)}, f32[768]{0:T(1024)}, u32[]{:S(2)}) copy-start(f32[768]{0:T(1024)} %get-tuple-element.424) | copy-start | bytes 9220
  442.4 68.2 %all-reduce.21.cloned.1.call-start = ((), (), s32[]{:S(2)}) async-start(), calls=%async_computation.8 | async-start | bytes 3145728 | tf_op jit(solution)/shard_map/psum | solution.py:251
  464.1 10.7 slice-start.8
  471.9 13.2 slice-start.4
  474.8 8.6 copy-start.8
  474.8 10.2 slice-start.5
  488.9 111.0 %all-reduce.23.cloned.1.call-start = ((), (), s32[]{:S(2)}) async-start(), calls=%async_computation.9 | async-start | bytes 3145728 | tf_op jit(solution)/shard_map/psum | solution.py:298
  489.0 10.7 copy-start.20
  578.2 8.3 copy-start.58
  578.2 65.3 %all-reduce.25.cloned.1.call-start = ((), (), s32[]{:S(2)}) async-start(), calls=%async_computation.10 | async-start | bytes 3145728 | tf_op jit(solution)/shard_map/psum | solution.py:251
  578.7 7.9 copy-start.17
  593.9 11.0 copy-start.94
  605.5 12.5 slice-start.6
  607.3 9.0 copy-start.6
  607.3 10.6 slice-start.7
  621.7 124.3 %all-reduce.27.cloned.1.call-start = ((), (), s32[]{:S(2)}) async-start(), calls=%async_computation.11 | async-start | bytes 3145728 | tf_op jit(solution)/shard_map/psum | solution.py:298
  627.4 7.5 copy-start.11
  627.4 7.5 copy-start.14
  627.4 7.5 copy-start.72
  627.4 7.5 copy-start.76
  639.8 7.9 copy-start.92
  661.4 19.9 %slice-start = ((s8[6291456]{0:T(1024)(128)(4,1)}), s8[2097152]{0:T(1024)(128)(4,1)S(1)}, s32[]{:S(2)}) async-start(s8[6291456]{0:T(1024)(128)(4,1)} %bitcast.387), calls=%async_computation.14 | async-start | bytes 4194304 | tf_op jit(solution)/shard_map/while
  669.0 12.3 slice-start.1
  688.5 19.9 %slice-start = ((s8[6291456]{0:T(1024)(128)(4,1)}), s8[2097152]{0:T(1024)(128)(4,1)S(1)}, s32[]{:S(2)}) async-start(s8[6291456]{0:T(1024)(128)(4,1)} %bitcast.387), calls=%async_computation.14 | async-start | bytes 4194304 | tf_op jit(solution)/shard_map/while
  696.1 12.3 slice-start.1
  724.3 8.8 copy-start.56
  724.3 763.8 %all-reduce.31.cloned.1.call-start = ((), (), s32[]{:S(2)}) async-start(), calls=%async_computation.13 | async-start | bytes 56623104 | tf_op jit(solution)/shard_map/psum | solution.py:328
  724.6 8.5 copy-start.25
  742.8 869.1 %all-reduce.29.cloned.1.call-start = ((), (), s32[]{:S(2)}) async-start(), calls=%async_computation.12 | async-start | bytes 135168 | tf_op jit(solution)/shard_map/psum | solution.py:342
  744.7 912.8 %copy-start.51 = (f32[2,48,384]{2,1,0:T(8,128)S(1)}, f32[2,48,384]{2,1,0:T(8,128)}, u32[]{:S(2)}) copy-start(f32[2,48,384]{2,1,0:T(8,128)} %param.30) | copy-start | bytes 442372
  744.7 912.8 %copy-start.73 = (f32[2,48,384]{2,1,0:T(8,128)S(1)}, f32[2,48,384]{2,1,0:T(8,128)}, u32[]{:S(2)}) copy-start(f32[2,48,384]{2,1,0:T(8,128)} %param.36) | copy-start | bytes 442372
  744.7 912.8 %copy-start.74 = (f32[2,48,384]{2,1,0:T(8,128)S(1)}, f32[2,48,384]{2,1,0:T(8,128)}, u32[]{:S(2)}) copy-start(f32[2,48,384]{2,1,0:T(8,128)} %param.37) | copy-start | bytes 442372
  750.6 908.7 %copy-start.34 = (f32[2,48,1536]{2,1,0:T(8,128)S(1)}, f32[2,48,1536]{2,1,0:T(8,128)}, u32[]{:S(2)}) copy-start(f32[2,48,1536]{2,1,0:T(8,128)} %param.31) | copy-start | bytes 1769476
  1488.1 173.3 %copy-start.32 = (f32[2,48,1536]{2,1,0:T(8,128)S(1)}, f32[2,48,1536]{2,1,0:T(8,128)}, u32[]{:S(2)}) copy-start(f32[2,48,1536]{2,1,0:T(8,128)} %param.32) | copy-start | bytes 1769476
  1661.4 47.4 %copy-start.43 = (f32[2,48,1536]{2,1,0:T(8,128)}, f32[2,48,1536]{2,1,0:T(8,128)S(1)}, u32[]{:S(2)}) copy-start(f32[2,48,1536]{2,1,0:T(8,128)S(1)} %get-tuple-element.528) | copy-start | bytes 1769476
  1661.4 47.4 %copy-start.44 = (f32[2,48,1536]{2,1,0:T(8,128)}, f32[2,48,1536]{2,1,0:T(8,128)S(1)}, u32[]{:S(2)}) copy-start(f32[2,48,1536]{2,1,0:T(8,128)S(1)} %get-tuple-element.529) | copy-start | bytes 1769476
  1667.0 45.7 %copy-start.49 = (f32[2,48,3,384]{3,1,2,0:T(8,128)}, f32[2,48,3,384]{3,1,2,0:T(8,128)S(1)}, u32[]{:S(2)}) copy-start(f32[2,48,3,384]{3,1,2,0:T(8,128)S(1)} %get-tuple-element.524) | copy-start | bytes 1327108
  (89 other events, 295.2 us)
Sparse Core Ops, SparseCore 0:
  11.3 73.9 all-gather.3
  88.5 54.6 all-gather.5
  146.7 19.2 all-reduce.12
  169.4 132.4 all-gather.7
  328.0 24.1 all-reduce.14
  392.3 21.5 all-reduce.16
  442.5 21.5 all-reduce.18
  489.0 21.5 all-reduce.20
  578.3 21.5 all-reduce.22
  621.9 21.5 all-reduce.24
  724.5 21.5 all-reduce.26
  752.4 735.7 all-reduce.30
  1495.2 116.6 all-reduce.28
